TPU v7x, 256 devices: a whole 4x4x8 slice. The times are simulated.
256 devices in a mesh: freq: 8 (over y, core), apt: 8 (over z), rcv: 4 (over x).
Axes of the slice: x: 4, y: 4, z: 8, core: 2. Of those that a mesh axis runs over, the one named last changes fastest.
Arguments:
- shot_lists: bfloat16 [256, 128, 8, 2, 128], P(('apt', 'rcv', 'freq')), may hold values from -6 to 6
- block_ids: int32 [256, 8], P(('apt', 'rcv')), may hold values from 0 to 15, all different within a row
- taper_ids: int32 [256, 8], P(('apt', 'rcv')), may hold values from 0 to 3
- green_traces: bfloat16 [128, 2, 2048, 2048], P('freq', None, 'apt', 'rcv'), may hold values from -0.1875 to 0.1875
Outputs:
- prediction: bfloat16 [256, 128, 2, 2048], P('apt', 'freq', None, 'rcv')
Inputs may be any that keep to these rules, and one draw needn't show every extreme that they name: `block_ids`: each output shot names 8 different aperture blocks, and every block is named by some shot.
All inputs are finite; a program needn't handle non-finite values.
Results may differ from a plain program's by a relative error of at most 0.015.
Values may be sent and summed in bfloat16 or wider, within the bound.
A program may use at most 128 MiB of HBM per device.

v0:
```python
import jax
import jax.numpy as jnp
from jax import lax
from jax.sharding import PartitionSpec as P


def windows(block_len):
    angles = jnp.pi * (jnp.arange(block_len, dtype=jnp.float32) + 0.5) / block_len
    cosine = jnp.cos(angles)
    return jnp.stack(
        [jnp.ones_like(cosine), 0.5 - 0.5 * cosine, 0.5 + 0.5 * cosine, jnp.sin(angles) ** 2],
        axis=0,
    )


def product(left, right):
    return jnp.einsum("sfk,fkr->sfr", left, right, preferred_element_type=jnp.float32)


def on_device(shot_lists, block_ids, taper_ids, green_traces):
    moved = lax.all_to_all(shot_lists, "freq", split_axis=1, concat_axis=0, tiled=True)
    block_len = moved.shape[-1]
    window_rows = windows(block_len)
    choose = (taper_ids[:, :, None] == jnp.arange(4, dtype=jnp.int32)).astype(jnp.float32)
    taper_rows = jnp.sum(choose[:, :, :, None] * window_rows[None, None, :, :], axis=2)
    tapered = (moved.astype(jnp.float32) * taper_rows[:, None, :, None, :]).astype(jnp.bfloat16)
    freq_count = tapered.shape[1]
    local_points = green_traces.shape[2]
    local_blocks = local_points // block_len
    gathered, gathered_ids = (
        lax.all_gather(tapered, ("apt", "rcv"), axis=0, tiled=True),
        lax.all_gather(block_ids, ("apt", "rcv"), axis=0, tiled=True),
    )
    first_block = lax.axis_index("apt") * local_blocks
    picked = (
        gathered_ids[:, :, None] == first_block + jnp.arange(local_blocks, dtype=jnp.int32)
    ).astype(jnp.bfloat16)
    aperture = jnp.einsum(
        "sjb,sfjct->sfcbt", picked, gathered, preferred_element_type=jnp.float32
    ).astype(jnp.bfloat16)
    aperture = aperture.reshape(-1, freq_count, 2, local_points)
    real_green = green_traces[:, 0]
    imag_green = green_traces[:, 1]
    real_part = aperture[:, :, 0]
    imag_part = aperture[:, :, 1]
    real_sum = product(real_part, real_green) - product(imag_part, imag_green)
    imag_sum = product(real_part, imag_green) + product(imag_part, real_green)
    return lax.psum_scatter(
        jnp.stack([real_sum, imag_sum], axis=2).astype(jnp.bfloat16),
        "apt",
        scatter_dimension=0,
        tiled=True,
    )


def solution(mesh):
    return jax.shard_map(
        on_device,
        mesh=mesh,
        in_specs=(
            P(("apt", "rcv", "freq"), None, None, None, None),
            P(("apt", "rcv"), None),
            P(("apt", "rcv"), None),
            P("freq", None, "apt", "rcv"),
        ),
        out_specs=P("apt", "freq", None, "rcv"),
        check_vma=False,
    )
```

profile of v0, /device:TPU:32, one launch (start us, length us, event | category | flops | bytes accessed | tf_op | source)
XLA Modules:
  0.0 338.7 jit_solution(13568734533111242891)
XLA Ops:
  6.5 0.0 copy-start.1
  6.5 4.6 %all-to-all-start = ((bf16[1,128,8,2,128]{4,3,2,0,1:T(2,128)(2,1)}), bf16[1,128,8,2,128]{4,3,2,0,1:T(2,128)(2,1)S(1)}, u32[]{:S(2)}, u32[]{:S(2)}) async-start(bf16[1,128,8,2,128]{4,3,2,0,1:T(2,128)(2,1)} %bitcast.47), calls=%async_computation | async-start | bytes 1048576 | tf_op jit(solution)/shard_map/all_to_all | solution.py:21
  11.1 0.0 all-gather.2.cloned.1.call-start
  11.2 0.1 broadcast_subtract_fusion
  11.3 0.1 pad_maximum_fusion.1
  11.4 0.7 fusion.24
  12.1 0.1 multiply_reduce_fusion
  12.2 9.3 %all-to-all-done = bf16[1,128,8,2,128]{4,3,2,0,1:T(2,128)(2,1)S(1)} async-done(((bf16[1,128,8,2,128]{4,3,2,0,1:T(2,128)(2,1)}), bf16[1,128,8,2,128]{4,3,2,0,1:T(2,128)(2,1)S(1)}, u32[]{:S(2)}, u32[]{:S(2)}) %all-to-all-start) | async-done | bytes 524320 | tf_op jit(solution)/shard_map/all_to_all | solution.py:21
  21.5 0.4 convert.13
  21.9 0.9 fusion.19
  22.8 0.0 all-gather.2.cloned.1.call-update
  22.8 0.0 reduce-scatter.2.cloned.1.call-start
  22.8 0.0 copy-done.1
  22.8 45.6 %all_gather.7 = s32[256,8]{1,0:T(8,128)S(1)} all-gather(s32[8,8]{1,0:T(8,128)S(1)} %copy-done.1), channel_id=1, replica_groups=mesh['freq'=8,'apt'=8,'rcv'=4] {'apt','rcv'}, dimensions={0}, use_global_device_ids=true | all-gather | bytes 8448 | tf_op jit(solution)/shard_map/all_gather | solution.py:32
  68.4 94.1 %all-gather.2.cloned.1.call-done = bf16[256,16,8,2,128]{4,2,3,1,0:T(8,128)(2,1)} async-done(((bf16[8,16,8,2,128]{4,2,3,1,0:T(8,128)(2,1)}), bf16[256,16,8,2,128]{4,2,3,1,0:T(8,128)(2,1)}) %all-gather.2.cloned.1.call-update) | async-done | bytes 16777232 | tf_op jit(solution)/shard_map/all_gather | solution.py:31
  162.5 10.6 %fusion = bf16[256,16,2,2,128]{4,3,2,1,0:T(2,128)(2,1)} fusion(bf16[256,16,8,2,128]{4,2,3,1,0:T(8,128)(2,1)} %all-gather.2.cloned.1.call-done, s32[256,8]{1,0:T(8,128)S(1)} %all_gather.7, s32[2]{0:T(128)S(1)} %iota_add_fusion), kind=kOutput, calls=%fused_computation.4 | convolution fusion | flops 35655680 | bytes 20979720 | tf_op jit(solution)/shard_map/sjb,sfjct->sfcbt/dot_general | solution.py:38
  173.1 11.7 %reshape.50 = bf16[256,16,2,256]{3,2,1,0:T(2,128)(2,1)} reshape(bf16[256,16,2,2,128]{4,3,2,1,0:T(2,128)(2,1)} %fusion) | data formatting | bytes 8388608 | tf_op jit(solution)/shard_map/reshape | solution.py:41
  184.8 11.1 %fusion.25 = (bf16[256,16,1,256]{3,2,1,0:T(2,128)(2,1)S(1)}, bf16[256,16,1,256]{3,2,1,0:T(2,128)(2,1)S(1)}) fusion(bf16[256,16,2,256]{3,2,1,0:T(2,128)(2,1)} %reshape.50), kind=kLoop, calls=%fused_computation.37 | loop fusion | bytes 8388608 | tf_op jit(solution)/shard_map/slice | solution.py:45
  195.9 0.0 copy-start
  195.9 9.8 %fusion.5 = f32[16,256,512]{2,1,0:T(8,128)} fusion(bf16[16,2,256,512]{3,2,1,0:T(8,128)(2,1)} %param.7, bf16[256,16,1,256]{3,2,1,0:T(2,128)(2,1)S(1)} %get-tuple-element.5), kind=kOutput, calls=%fused_computation.9 | convolution fusion | flops 1073741824 | bytes 14680064 | tf_op jit(solution)/shard_map/sfk,fkr->sfr/dot_general | solution.py:17
  205.7 0.0 copy-done
  205.7 5.0 %fusion.3 = f32[16,256,512]{2,1,0:T(8,128)S(1)} fusion(bf16[16,2,256,512]{3,2,1,0:T(8,128)(2,1)} %param.7, bf16[256,16,1,256]{3,2,1,0:T(2,128)(2,1)S(1)} %get-tuple-element.6), kind=kOutput, calls=%fused_computation.7 | convolution fusion | flops 1073741824 | bytes 14680064 | tf_op jit(solution)/shard_map/sfk,fkr->sfr/dot_general | solution.py:17
  210.7 10.8 %fusion.1 = bf16[256,16,1,512]{3,0,1,2:T(8,128)(2,1)} fusion(f32[16,256,512]{2,1,0:T(8,128)} %fusion.5, bf16[16,2,256,512]{3,2,1,0:T(8,128)(2,1)} %param.7, bf16[256,16,1,256]{3,2,1,0:T(2,128)(2,1)} %copy-done), kind=kOutput, calls=%fused_computation.5 | convolution fusion | flops 1077936128 | bytes 20971520 | tf_op jit(solution)/shard_map/sfk,fkr->sfr/dot_general | solution.py:17
  221.6 7.3 %fusion.2 = bf16[256,16,1,512]{3,0,1,2:T(8,128)(2,1)} fusion(f32[16,256,512]{2,1,0:T(8,128)S(1)} %fusion.3, bf16[16,2,256,512]{3,2,1,0:T(8,128)(2,1)} %param.7, bf16[256,16,1,256]{3,2,1,0:T(2,128)(2,1)S(1)} %get-tuple-element.5), kind=kOutput, calls=%fused_computation.6 | convolution fusion | flops 1077936128 | bytes 18874368 | tf_op jit(solution)/shard_map/sfk,fkr->sfr/dot_general | solution.py:17
  228.9 7.5 %pad_maximum_fusion = bf16[256,16,2,512]{3,0,1,2:T(8,128)(2,1)} fusion(bf16[256,16,1,512]{3,0,1,2:T(8,128)(2,1)} %fusion.2, bf16[256,16,1,512]{3,0,1,2:T(8,128)(2,1)} %fusion.1), kind=kLoop, calls=%fused_computation | loop fusion | flops 4194304 | bytes 16777216 | tf_op jit(solution)/shard_map/stack | solution.py:49
  236.4 0.0 reduce-scatter.2.cloned.1.call-update
  236.4 92.2 %reduce-scatter.2.cloned.1.call-done = bf16[32,16,2,512]{3,0,1,2:T(8,128)(2,1)} async-done(((bf16[256,16,2,512]{3,0,1,2:T(8,128)(2,1)}), bf16[32,16,2,512]{3,0,1,2:T(8,128)(2,1)}) %reduce-scatter.2.cloned.1.call-update) | async-done | bytes 1048592 | tf_op jit(solution)/shard_map/reduce_scatter | solution.py:48
  328.6 3.3 copy.24
  (3 shorter events, 0.1 us)
Async XLA Ops:
  6.5 16.3 %copy-start.1 = (s32[8,8]{1,0:T(8,128)S(1)}, s32[8,8]{1,0:T(8,128)}, u32[]{:S(2)}) copy-start(s32[8,8]{1,0:T(8,128)} %param.5) | copy-start | bytes 772
  6.5 15.0 %all-to-all-start = ((bf16[1,128,8,2,128]{4,3,2,0,1:T(2,128)(2,1)}), bf16[1,128,8,2,128]{4,3,2,0,1:T(2,128)(2,1)S(1)}, u32[]{:S(2)}, u32[]{:S(2)}) async-start(bf16[1,128,8,2,128]{4,3,2,0,1:T(2,128)(2,1)} %bitcast.47), calls=%async_computation | async-start | bytes 1048576 | tf_op jit(solution)/shard_map/all_to_all | solution.py:21
  11.1 151.3 %all-gather.2.cloned.1.call-start = ((), (), s32[]{:S(2)}) async-start(), calls=%async_computation.2 | async-start | bytes 17301504 | tf_op jit(solution)/shard_map/all_gather | solution.py:31
  22.8 305.8 %reduce-scatter.2.cloned.1.call-start = ((), (), s32[]{:S(2)}) async-start(), calls=%async_computation.3 | async-start | bytes 9437184 | tf_op jit(solution)/shard_map/reduce_scatter | solution.py:48
  195.9 9.8 %copy-start = (bf16[256,16,1,256]{3,2,1,0:T(2,128)(2,1)}, bf16[256,16,1,256]{3,2,1,0:T(2,128)(2,1)S(1)}, u32[]{:S(2)}) copy-start(bf16[256,16,1,256]{3,2,1,0:T(2,128)(2,1)S(1)} %get-tuple-element.6) | copy-start | bytes 6291460
Sparse Core Ops, SparseCore 0:
  22.9 139.5 all-gather.1
  236.5 92.0 reduce-scatter.1
where the time goes:
time: 342 us; the launch traced here: 339 us
  waiting for transfers between devices  196 us (57%)
  blocking collectives  45.6 us (13%)
  matrix products  43.6 us (13%)
  local copies, waits for them, and re-layouts  26.1 us (8%)
  between operations  13.5 us (4%)
  other arithmetic  9.68 us (3%)
  starting transfers between devices  4.68 us (1%)
    all_gather x1, waiting for transfers between devices, on_device(): lax.all_gather(tapered, ('apt', 'rcv'), axis=0, tiled=True)  94.1 us
    reduce_scatter x1, waiting for transfers between devices, on_device(): lax.psum_scatter(jnp.stack([real_sum, imag_sum], axis=2).astype(jnp.bfloa...  92.2 us
    all_gather x1, blocking collectives, on_device(): lax.all_gather(block_ids, ('apt', 'rcv'), axis=0, tiled=True)  45.6 us
    dot_general x4, matrix products, product(): jnp.einsum('sfk,fkr->sfr', left, right, preferred_element_type=jnp.float32)  33 us
    reshape x1, local copies, waits for them, and re-layouts, on_device(): aperture = aperture.reshape(-1, freq_count, 2, local_points)  11.7 us
    slice x1, local copies, waits for them, and re-layouts, on_device(): imag_part = aperture[:, :, 1]  11.1 us
    dot_general x1, matrix products, on_device(): jnp.einsum('sjb,sfjct->sfcbt', picked, gathered, preferred_element_type=j...  10.6 us
    all_to_all x1, waiting for transfers between devices, on_device(): lax.all_to_all(shot_lists, 'freq', split_axis=1, concat_axis=0, tiled=True)  9.32 us
  transfers between devices with their start and end apart: 3, of which 3 were waited for; matrix products, arithmetic and copies ran while one was open for 0% of the time, Pallas kernels for 0%

commit v1 on v0

v1 whole, which is shorter than its diff:
```python
import functools

import jax
import jax.numpy as jnp
from jax import lax
from jax.experimental import pallas as pl
from jax.experimental.pallas import tpu as pltpu
from jax.sharding import PartitionSpec as P

MESH = pl.DeviceIdType.MESH
CHUNKS = 4
SKEW = 4
EARLY = 3


def windows(block_len):
    angles = jnp.pi * (jnp.arange(block_len, dtype=jnp.float32) + 0.5) / block_len
    cosine = jnp.cos(angles)
    return jnp.stack(
        [jnp.ones_like(cosine), 0.5 - 0.5 * cosine, 0.5 + 0.5 * cosine, jnp.sin(angles) ** 2],
        axis=0,
    )


def kernel(
    sizes,
    lists,
    taper,
    select,
    green,
    out,
    raw,
    dense,
    apert,
    held_green,
    partial,
    ring,
    green_sem,
    y_send,
    y_recv,
    z_send,
    z_recv,
    x_send,
    x_recv,
    own_sem,
    ring_send,
    ring_recv,
):
    n_freq, n_apt, n_rcv = sizes
    me_f, me_z, me_x = lax.axis_index("freq"), lax.axis_index("apt"), lax.axis_index("rcv")
    freqs = held_green.shape[0]
    per = freqs // CHUNKS
    steps = n_apt

    barrier = pltpu.get_barrier_semaphore()

    def greet(axis, me, size):
        @pl.loop(1, size)
        def _(off):
            pl.semaphore_signal(
                barrier, inc=1, device_id={axis: lax.rem(me + off, size)}, device_id_type=MESH
            )

    def green_copy(f):
        return pltpu.make_async_copy(green.at[f], held_green.at[f], green_sem.at[f])

    greet("freq", me_f, n_freq)
    greet("apt", me_z, n_apt)
    greet("rcv", me_x, n_rcv)

    def own_lists(c):
        return pltpu.make_async_copy(
            lists.at[pl.ds(me_f * freqs + c * per, per)],
            raw.at[me_f, pl.ds(c * per, per)],
            own_sem.at[0, c],
        )

    @pl.loop(0, CHUNKS)
    def _(c):
        own_lists(c).start()

    pl.semaphore_wait(barrier, n_freq + n_apt + n_rcv - 3)

    def y_copy(c, off):
        peer = lax.rem(me_f + off, n_freq)
        return pltpu.make_async_remote_copy(
            src_ref=lists.at[pl.ds(peer * freqs + c * per, per)],
            dst_ref=raw.at[me_f, pl.ds(c * per, per)],
            send_sem=y_send.at[c, off],
            recv_sem=y_recv.at[c, off],
            device_id={"freq": peer},
            device_id_type=MESH,
        )

    def z_copy(c, off):
        peer = lax.rem(me_z + off, n_apt)
        return pltpu.make_async_remote_copy(
            src_ref=dense.at[pl.ds(c * per, per), peer],
            dst_ref=apert.at[pl.ds(c * per, per), me_z, me_x],
            send_sem=z_send.at[c, off],
            recv_sem=z_recv.at[c, off],
            device_id={"apt": peer},
            device_id_type=MESH,
        )

    def own_dense(c):
        return pltpu.make_async_copy(
            dense.at[pl.ds(c * per, per), me_z],
            apert.at[pl.ds(c * per, per), me_z, me_x],
            own_sem.at[1, c],
        )

    def x_copy(c, off):
        peer = lax.rem(me_x + off, n_rcv)
        mine = apert.at[pl.ds(c * per, per), :, me_x]
        return pltpu.make_async_remote_copy(
            src_ref=mine,
            dst_ref=mine,
            send_sem=x_send.at[c, off],
            recv_sem=x_recv.at[c, off],
            device_id={"rcv": peer},
            device_id_type=MESH,
        )

    def ring_copy(f, t, way):
        goal = lax.rem(me_z - way * (1 + t) + 2 * n_apt, n_apt)
        return pltpu.make_async_remote_copy(
            src_ref=partial.at[f, goal],
            dst_ref=ring.at[f, t],
            send_sem=ring_send.at[f, t],
            recv_sem=ring_recv.at[f, t],
            device_id={"apt": lax.rem(me_z + way + n_apt, n_apt)},
            device_id_type=MESH,
        )

    @pl.loop(0, CHUNKS)
    def _(c):
        @pl.loop(1, n_freq)
        def _(off):
            y_copy(c, off).start()

    @pl.loop(0, freqs)
    def _(f):
        green_copy(f).start()

    @pl.loop(0, CHUNKS)
    def _(c):
        own_lists(c).wait()

        @pl.loop(1, n_freq)
        def _(off):
            y_copy(c, off).wait_recv()

        @pl.loop(0, per)
        def _(i):
            f = c * per + i
            rows = raw[:, f]
            rows = rows.reshape(taper.shape).astype(jnp.float32) * taper[...]
            placed = jnp.dot(
                select[...], rows.astype(jnp.bfloat16), preferred_element_type=jnp.float32
            )
            dense[f] = placed.astype(jnp.bfloat16).reshape(dense.shape[1:])

        own_dense(c).start()

        @pl.loop(1, n_apt)
        def _(off):
            z_copy(c, off).start()

    def spread(c):
        own_dense(c).wait()

        @pl.loop(1, n_apt)
        def _(off):
            z_copy(c, off).wait_recv()

        @pl.loop(1, n_rcv)
        def _(off):
            x_copy(c, off).start()

    @pl.loop(0, EARLY)
    def _(c):
        spread(c)

    def multiply(f):
        green_copy(f).wait()
        blocks = apert.shape[3]
        depth = apert.shape[5]
        rows = apert.shape[1] * apert.shape[2] * apert.shape[4]
        left = jnp.concatenate([apert[f, :, :, b].reshape(rows, depth) for b in range(blocks)], axis=1)
        wide = left.astype(jnp.float32).reshape(rows // 8, 8, blocks * depth)
        odd = lax.rem(lax.broadcasted_iota(jnp.int32, wide.shape, 1), 2) == 1
        turned = jnp.where(odd, pltpu.roll(wide, 1, 1), -pltpu.roll(wide, 7, 1))
        turned = turned.reshape(rows, blocks * depth).astype(jnp.bfloat16)
        both = jnp.concatenate([left, turned], axis=1)
        right = held_green[f].reshape(2 * held_green.shape[2], held_green.shape[3])
        sums = jnp.dot(both, right, preferred_element_type=jnp.float32)
        partial[f] = sums.astype(jnp.bfloat16).reshape(partial.shape[1:])

    def advance(f, t, way):
        goal = lax.rem(me_z - way * (1 + t) + 2 * n_apt, n_apt)
        ring_copy(f, t - 1, way).wait_recv()
        return goal, (
            ring[f, t - 1].astype(jnp.float32) + partial[f, goal].astype(jnp.float32)
        ).astype(jnp.bfloat16)

    @pl.loop(0, steps + SKEW * (CHUNKS - 1))
    def _(tick):
        @pl.loop(0, CHUNKS)
        def _(c):
            t = tick - SKEW * c

            @pl.when(t == 0)
            def _():
                @pl.loop(1, n_rcv)
                def _(off):
                    x_copy(c, off).wait_recv()

                @pl.loop(0, per // 2)
                def _(i):
                    f = c * per + 2 * i
                    multiply(f)
                    ring_copy(f, 0, 1).start()
                    multiply(f + 1)
                    ring_copy(f + 1, 0, -1).start()

            @pl.when(jnp.logical_and(t > 0, t < steps - 1))
            def _():
                @pl.loop(0, per // 2)
                def _(i):
                    for way in (1, -1):
                        f = c * per + 2 * i + (1 - way) // 2
                        goal, value = advance(f, t, way)
                        partial[f, goal] = value
                        ring_copy(f, t, way).start()

            @pl.when(t == steps - 1)
            def _():
                @pl.loop(0, per // 2)
                def _(i):
                    for way in (1, -1):
                        f = c * per + 2 * i + (1 - way) // 2
                        out[f] = advance(f, t, way)[1]

        for c in range(EARLY, CHUNKS):
            @pl.when(tick == c - EARLY)
            def _():
                spread(c)

    @pl.loop(0, CHUNKS)
    def _(c):
        @pl.loop(1, n_freq)
        def _(off):
            y_copy(c, off).wait_send()

        @pl.loop(1, n_apt)
        def _(off):
            z_copy(c, off).wait_send()

        @pl.loop(1, n_rcv)
        def _(off):
            x_copy(c, off).wait_send()

    @pl.loop(0, freqs)
    def _(f):
        @pl.loop(0, steps - 1)
        def _(t):
            ring_copy(f, t, 1).wait_send()


def on_device(sizes, shot_lists, block_ids, taper_ids, green_traces):
    n_freq, n_apt, n_rcv = sizes
    _, all_freqs, entries, parts, length = shot_lists.shape
    shots = block_ids.shape[0]
    freqs, _, points, width = green_traces.shape
    blocks = points // length
    lists = shot_lists.reshape(all_freqs, entries * parts, length)

    choose = (taper_ids[:, :, None] == jnp.arange(4, dtype=jnp.int32)).astype(jnp.float32)
    taper = jnp.sum(choose[:, :, :, None] * windows(length)[None, None, :, :], axis=2)
    taper = jnp.broadcast_to(taper[:, :, None, :], (shots, entries, parts, length))
    taper = taper.reshape(shots * entries * parts, length)

    rows, columns = n_apt * blocks * shots * parts, shots * entries * parts
    row, column = jnp.arange(rows)[:, None], jnp.arange(columns)[None, :]
    named = jnp.broadcast_to(block_ids[:, :, None], (shots, entries, parts)).reshape(1, columns)
    select = (
        (row // (shots * parts) == named)
        & (row // parts % shots == column // (entries * parts))
        & (row % parts == column % parts)
    ).astype(jnp.bfloat16)

    tile = shots * parts
    result = pl.pallas_call(
        functools.partial(kernel, sizes),
        out_shape=jax.ShapeDtypeStruct((freqs, n_rcv * tile, width), jnp.bfloat16),
        in_specs=[
            pl.BlockSpec(memory_space=pl.ANY),
            pl.BlockSpec(memory_space=pltpu.VMEM),
            pl.BlockSpec(memory_space=pltpu.VMEM),
            pl.BlockSpec(memory_space=pl.ANY),
        ],
        out_specs=pl.BlockSpec(memory_space=pltpu.VMEM),
        scratch_shapes=[
            pltpu.VMEM((shots, freqs, entries * parts, length), jnp.bfloat16),
            pltpu.VMEM((freqs, n_apt, blocks, tile, length), jnp.bfloat16),
            pltpu.VMEM((freqs, n_apt, n_rcv, blocks, tile, length), jnp.bfloat16),
            pltpu.VMEM((freqs, parts, points, width), jnp.bfloat16),
            pltpu.VMEM((freqs, n_apt, n_rcv * tile, width), jnp.bfloat16),
            pltpu.VMEM((freqs, n_apt - 1, n_rcv * tile, width), jnp.bfloat16),
            pltpu.SemaphoreType.DMA((freqs,)),
            pltpu.SemaphoreType.DMA((CHUNKS, n_freq)),
            pltpu.SemaphoreType.DMA((CHUNKS, n_freq)),
            pltpu.SemaphoreType.DMA((CHUNKS, n_apt)),
            pltpu.SemaphoreType.DMA((CHUNKS, n_apt)),
            pltpu.SemaphoreType.DMA((CHUNKS, n_rcv)),
            pltpu.SemaphoreType.DMA((CHUNKS, n_rcv)),
            pltpu.SemaphoreType.DMA((2, CHUNKS)),
            pltpu.SemaphoreType.DMA((freqs, n_apt - 1)),
            pltpu.SemaphoreType.DMA((freqs, n_apt - 1)),
        ],
        compiler_params=pltpu.CompilerParams(
            collective_id=0, has_side_effects=True, vmem_limit_bytes=52 * 1024 * 1024
        ),
    )(lists, taper, select, green_traces)
    return result.reshape(freqs, n_rcv * shots, parts, width).transpose(1, 0, 2, 3)


def solution(mesh):
    sizes = (mesh.shape["freq"], mesh.shape["apt"], mesh.shape["rcv"])
    return jax.shard_map(
        functools.partial(on_device, sizes),
        mesh=mesh,
        in_specs=(
            P(("apt", "rcv", "freq"), None, None, None, None),
            P(("apt", "rcv"), None),
            P(("apt", "rcv"), None),
            P("freq", None, "apt", "rcv"),
        ),
        out_specs=P("apt", "freq", None, "rcv"),
        check_vma=False,
    )
```

time: 342 us -> 141 us (0.41)
  waiting for transfers between devices: 196 us -> 0 us
  Pallas kernels: 0 us -> 133 us
  blocking collectives: 45.6 us -> 0 us
  matrix products: 43.6 us -> 0 us
  local copies, waits for them, and re-layouts: 26.1 us -> 4.49 us
  between operations: 13.5 us -> 0.06 us
  other arithmetic: 9.68 us -> 1.15 us
  starting transfers between devices: 4.68 us -> 0 us
    pallas_call x0 -> x1, Pallas kernels: none -> 133 us  [on_device(): pl.pallas_call(functools.partial(kernel, sizes), out_shape=jax.ShapeDtype...]
    all_gather x1 -> x0, waiting for transfers between devices: 94.1 us -> none  [on_device(): lax.all_gather(tapered, ('apt', 'rcv'), axis=0, tiled=True)]
    reduce_scatter x1 -> x0, waiting for transfers between devices: 92.2 us -> none  [on_device(): lax.psum_scatter(jnp.stack([real_sum, imag_sum], axis=2).astype(jnp.bfloa...]
    all_gather x1 -> x0, blocking collectives: 45.6 us -> none  [on_device(): lax.all_gather(block_ids, ('apt', 'rcv'), axis=0, tiled=True)]
    dot_general x5 -> x0, matrix products: 43.6 us -> none  [the longest x4 33 us: product(): jnp.einsum('sfk,fkr->sfr', left, right, preferred_element_type=jnp.float32)]
    slice x1 -> x0, local copies, waits for them, and re-layouts: 11.1 us -> none  [on_device(): imag_part = aperture[:, :, 1]]
    all_to_all x1 -> x0, waiting for transfers between devices: 9.32 us -> none  [on_device(): lax.all_to_all(shot_lists, 'freq', split_axis=1, concat_axis=0, tiled=True)]
    reshape x1 -> x2, local copies, waits for them, and re-layouts: 11.7 us -> 2.52 us  [on_device(): result.reshape(freqs, n_rcv * shots, parts, width).transpose(1, 0, 2, 3)]
  transfers between devices with their start and end apart: 3 -> 0, of which waited for: 3 -> 0; matrix products, arithmetic and copies ran while one was open for 0% -> 0% of each run, Pallas kernels for 0% -> 0%
where the time goes in v1:
time: 141 us; the launch traced here: 139 us
  Pallas kernels  133 us (94%)
  local copies, waits for them, and re-layouts  4.49 us (3%)
    pallas_call x1, Pallas kernels, on_device(): pl.pallas_call(functools.partial(kernel, sizes), out_shape=jax.ShapeDtype...  133 us

profile of v1, /device:TPU:32, one launch (start us, length us, event | category | flops | bytes accessed | tf_op | source)
XLA Modules:
  0.0 139.1 jit_solution(13678060343259502432)
XLA Ops:
  0.1 0.1 sine_multiply_fusion
  0.1 0.1 pad_maximum_fusion
  0.2 0.7 fusion
  0.9 0.1 multiply_reduce_fusion
  1.0 0.8 broadcast_in_dim.5
  1.8 0.1 eq.67
  1.9 0.2 and_convert_fusion.select
  2.1 0.0 copy-start
  2.1 1.0 copy-done
  3.2 133.4 %shard_map.46 = bf16[16,64,512]{2,1,0:T(8,128)(2,1)S(1)} custom-call(bf16[128,16,128]{2,1,0:T(8,128)(2,1)S(1)} %bitcast.6, f32[128,128]{1,0:T(8,128)S(1)} %bitcast.7, bf16[256,128]{1,0:T(8,128)(2,1)S(1)} %and_convert_fusion.select, bf16[16,2,256,512]{3,2,1,0:T(8,128)(2,1)} %green.1), custom_call_target="tpu_custom_call" | custom-call | tf_op jit(solution)/shard_map/pallas_call | solution.py:294
  136.6 0.4 reshape.204
  137.0 2.1 %copy.9 = bf16[16,32,2,512]{3,2,0,1:T(2,128)(2,1)} copy(bf16[16,32,2,512]{3,2,1,0:T(2,128)(2,1)S(1)} %reshape.204) | data formatting | bytes 2097152 | tf_op jit(solution)/shard_map/reshape | solution.py:326
  (6 shorter events, 0.1 us)
Async XLA Ops:
  2.1 1.0 copy-start

commit v2 on v0

v2 whole, which is shorter than its diff:
```python
import functools

import jax
import jax.numpy as jnp
from jax import lax
from jax.experimental import pallas as pl
from jax.experimental.pallas import tpu as pltpu
from jax.sharding import PartitionSpec as P

MESH = pl.DeviceIdType.MESH
CHUNKS = (2, 2, 2, 2, 4, 4)
PLAN = (
    "D0", "D1", "D2", "D4", "X0", "X1", "F0", "X2", "D3", "M0", "D5", "F1", "F2", "X3",
    "M1", "X4", "M2", "X5", "T", "F3", "T", "F4", "T", "F5", "M3", "T", "M6", "M7",
    "M4", "M5",
)


def windows(block_len):
    angles = jnp.pi * (jnp.arange(block_len, dtype=jnp.float32) + 0.5) / block_len
    cosine = jnp.cos(angles)
    return jnp.stack(
        [jnp.ones_like(cosine), 0.5 - 0.5 * cosine, 0.5 + 0.5 * cosine, jnp.sin(angles) ** 2],
        axis=0,
    )


def kernel(
    sizes,
    listed,
    ids,
    tapers,
    shape,
    green,
    out,
    named_ids,
    named_tapers,
    lists,
    raw,
    taper,
    select,
    dense,
    apert,
    held_green,
    partial,
    ring,
    load_sem,
    green_sem,
    own_sem,
    y_send,
    y_recv,
    z_send,
    z_recv,
    x_send,
    x_recv,
    ring_send,
    ring_recv,
):
    n_freq, n_apt, n_rcv = sizes
    me_f, me_z, me_x = lax.axis_index("freq"), lax.axis_index("apt"), lax.axis_index("rcv")
    freqs = held_green.shape[0]
    entries = named_ids.shape[1]
    last = n_apt - 1
    starts = [sum(CHUNKS[:c]) for c in range(len(CHUNKS))]

    loads = [
        pltpu.make_async_copy(source, target, load_sem.at[k])
        for k, (source, target) in enumerate(
            ((listed, lists), (ids, named_ids), (tapers, named_tapers))
        )
    ]
    for load in loads:
        load.start()

    barrier = pltpu.get_barrier_semaphore()
    for axis, me, size in (("freq", me_f, n_freq), ("apt", me_z, n_apt), ("rcv", me_x, n_rcv)):
        if axis == "rcv":
            offsets = (1, size - 1)
            for off in offsets:
                pl.semaphore_signal(
                    barrier, inc=1, device_id={axis: lax.rem(me + off, size)}, device_id_type=MESH
                )
        else:
            @pl.loop(1, size)
            def _(off):
                pl.semaphore_signal(
                    barrier, inc=1, device_id={axis: lax.rem(me + off, size)}, device_id_type=MESH
                )

    def span(c):
        return pl.ds(starts[c], CHUNKS[c])

    def own_lists(c):
        return pltpu.make_async_copy(
            lists.at[pl.ds(me_f * freqs + starts[c], CHUNKS[c])],
            raw.at[me_f, span(c)],
            own_sem.at[0, c],
        )

    def own_dense(c):
        return pltpu.make_async_copy(
            dense.at[span(c), me_z], apert.at[span(c), me_z, me_x], own_sem.at[1, c]
        )

    def green_copy(f):
        return pltpu.make_async_copy(green.at[f], held_green.at[f], green_sem.at[f])

    def y_copy(c, off):
        peer = lax.rem(me_f + off, n_freq)
        return pltpu.make_async_remote_copy(
            src_ref=lists.at[pl.ds(peer * freqs + starts[c], CHUNKS[c])],
            dst_ref=raw.at[me_f, span(c)],
            send_sem=y_send.at[c, off],
            recv_sem=y_recv.at[c, off],
            device_id={"freq": peer},
            device_id_type=MESH,
        )

    def z_copy(c, off):
        peer = lax.rem(me_z + off, n_apt)
        return pltpu.make_async_remote_copy(
            src_ref=dense.at[span(c), peer],
            dst_ref=apert.at[span(c), me_z, me_x],
            send_sem=z_send.at[c, off],
            recv_sem=z_recv.at[c, off],
            device_id={"apt": peer},
            device_id_type=MESH,
        )

    def x_copy(c, kind):
        way = (1, -1)[kind % 2]
        if kind < 2:
            block = apert.at[span(c), :, me_x]
        else:
            part = CHUNKS[c] // 2
            which = pl.ds(starts[c] + (part if way < 0 else 0), part)
            block = apert.at[which, :, lax.rem(me_x - way + n_rcv, n_rcv)]
        return pltpu.make_async_remote_copy(
            src_ref=block,
            dst_ref=block,
            send_sem=x_send.at[c, kind],
            recv_sem=x_recv.at[c, kind],
            device_id={"rcv": lax.rem(me_x + way + n_rcv, n_rcv)},
            device_id_type=MESH,
        )

    def goal_of(t, way):
        return lax.rem(me_z - way * (1 + t) + 2 * n_apt, n_apt)

    def ring_copy(p, t, way):
        turn = (1 - way) // 2
        return pltpu.make_async_remote_copy(
            src_ref=partial.at[2 * p + turn, goal_of(t, way)],
            dst_ref=ring.at[t, 2 * p + turn],
            send_sem=ring_send.at[p, t, turn],
            recv_sem=ring_recv.at[p, t, turn],
            device_id={"apt": lax.rem(me_z + way + n_apt, n_apt)},
            device_id_type=MESH,
        )

    loads[0].wait()
    pl.semaphore_wait(barrier, n_freq + n_apt)
    for c in range(len(CHUNKS)):
        @pl.loop(1, n_freq)
        def _(off):
            y_copy(c, off).start()

        own_lists(c).start()

    @pl.loop(0, freqs)
    def _(f):
        green_copy(f).start()

    loads[1].wait()
    loads[2].wait()
    rows, columns = select.shape
    tile = 2 * n_freq
    row = lax.broadcasted_iota(jnp.int32, (rows, columns), 0)
    column = lax.broadcasted_iota(jnp.int32, (8, columns), 1)
    strip_row = lax.broadcasted_iota(jnp.int32, taper.shape, 0) // 2
    named = jnp.zeros((8, columns), jnp.int32)
    chosen = jnp.zeros(taper.shape, jnp.int32)
    for k in range(n_freq * entries):
        named = jnp.where(column // 2 == k, named_ids[k // entries, k % entries], named)
        chosen = jnp.where(strip_row == k, named_tapers[k // entries, k % entries], chosen)
    goal_row = named * tile + column // (2 * entries) * 2 + column % 2
    hit = row == jnp.broadcast_to(goal_row[0:1], (rows, columns))
    select[...] = jnp.where(hit, 1.0, 0.0).astype(jnp.bfloat16)
    weights = jnp.broadcast_to(shape[0:1, :], taper.shape)
    for w in range(1, 4):
        weights = jnp.where(chosen == w, jnp.broadcast_to(shape[w : w + 1, :], taper.shape), weights)
    taper[...] = weights

    def place(c):
        own_lists(c).wait()

        @pl.loop(1, n_freq)
        def _(off):
            y_copy(c, off).wait_recv()

        @pl.loop(0, CHUNKS[c])
        def _(i):
            f = starts[c] + i
            weighed = raw[:, f].reshape(taper.shape).astype(jnp.float32) * taper[...]
            placed = jnp.dot(
                select[...], weighed.astype(jnp.bfloat16), preferred_element_type=jnp.float32
            )
            dense[f] = placed.astype(jnp.bfloat16).reshape(dense.shape[1:])

        @pl.loop(1, n_apt)
        def _(off):
            z_copy(c, off).start()

        own_dense(c).start()

    def spread(c):
        own_dense(c).wait()

        @pl.loop(1, n_apt)
        def _(off):
            z_copy(c, off).wait_recv()

        x_copy(c, 0).start()
        x_copy(c, 1).start()

    def forward(c):
        x_copy(c, 0).wait_recv()
        x_copy(c, 2).start()
        x_copy(c, 1).wait_recv()
        x_copy(c, 3).start()

    gathered = set()

    def multiply(p):
        c = max(k for k, start in enumerate(starts) if start <= 2 * p)
        if c not in gathered:
            gathered.add(c)
            x_copy(c, 2).wait_recv()
            x_copy(c, 3).wait_recv()
        blocks, depth = apert.shape[3], apert.shape[5]
        count = n_apt * n_rcv * tile
        for way in (1, -1):
            f = 2 * p + (1 - way) // 2
            green_copy(f).wait()
            left = jnp.concatenate(
                [apert[f, :, :, b].reshape(count, depth) for b in range(blocks)], axis=1
            )
            wide = left.astype(jnp.float32).reshape(count // 8, 8, blocks * depth)
            odd = lax.rem(lax.broadcasted_iota(jnp.int32, wide.shape, 1), 2) == 1
            turned = jnp.where(odd, pltpu.roll(wide, 1, 1), -pltpu.roll(wide, 7, 1))
            turned = turned.reshape(count, blocks * depth).astype(jnp.bfloat16)
            both = jnp.concatenate([left, turned], axis=1)
            right = held_green[f].reshape(2 * held_green.shape[2], held_green.shape[3])
            sums = jnp.dot(both, right, preferred_element_type=jnp.float32)
            partial[f] = sums.astype(jnp.bfloat16).reshape(partial.shape[1:])
            ring_copy(p, 0, way).start()

    def advance(p, t):
        for way in (1, -1):
            f = 2 * p + (1 - way) // 2
            ring_copy(p, t - 1, way).wait_recv()
            goal = goal_of(t, way)
            value = ring[t - 1, f] + partial[f, goal]
            if t < last:
                partial[f, goal] = value
                ring_copy(p, t, way).start()
            else:
                out[f] = value

    going = {}

    def tick():
        for p in list(going):
            going[p] += 1
            advance(p, going[p])
            if going[p] == last:
                del going[p]

    for event in PLAN:
        if event == "T":
            tick()
        else:
            {"D": place, "X": spread, "F": forward, "M": multiply}[event[0]](int(event[1]))
            if event[0] == "M":
                going[int(event[1])] = 0
    while going:
        tick()

    for c in range(len(CHUNKS)):
        @pl.loop(1, n_freq)
        def _(off):
            y_copy(c, off).wait_send()

        @pl.loop(1, n_apt)
        def _(off):
            z_copy(c, off).wait_send()

        for kind in range(4):
            x_copy(c, kind).wait_send()

    @pl.loop(0, freqs // 2)
    def _(p):
        @pl.loop(0, last)
        def _(t):
            for way in (1, -1):
                ring_copy(p, t, way).wait_send()


def on_device(sizes, shot_lists, block_ids, taper_ids, green_traces):
    n_freq, n_apt, n_rcv = sizes
    _, all_freqs, entries, parts, length = shot_lists.shape
    shots = block_ids.shape[0]
    freqs, _, points, width = green_traces.shape
    blocks = points // length
    lists = shot_lists.reshape(all_freqs, entries * parts, length)
    tile = shots * parts
    chunks = len(CHUNKS)
    dma = pltpu.SemaphoreType.DMA
    result = pl.pallas_call(
        functools.partial(kernel, sizes),
        out_shape=jax.ShapeDtypeStruct((freqs, n_rcv * tile, width), jnp.bfloat16),
        in_specs=[
            pl.BlockSpec(memory_space=pl.ANY),
            pl.BlockSpec(memory_space=pl.ANY),
            pl.BlockSpec(memory_space=pl.ANY),
            pl.BlockSpec(memory_space=pltpu.VMEM),
            pl.BlockSpec(memory_space=pl.ANY),
        ],
        out_specs=pl.BlockSpec(memory_space=pltpu.VMEM),
        scratch_shapes=[
            pltpu.SMEM(block_ids.shape, jnp.int32),
            pltpu.SMEM(taper_ids.shape, jnp.int32),
            pltpu.VMEM(lists.shape, jnp.bfloat16),
            pltpu.VMEM((shots, freqs, entries * parts, length), jnp.bfloat16),
            pltpu.VMEM((shots * entries * parts, length), jnp.float32),
            pltpu.VMEM((n_apt * blocks * tile, shots * entries * parts), jnp.bfloat16),
            pltpu.VMEM((freqs, n_apt, blocks, tile, length), jnp.bfloat16),
            pltpu.VMEM((freqs, n_apt, n_rcv, blocks, tile, length), jnp.bfloat16),
            pltpu.VMEM((freqs, parts, points, width), jnp.bfloat16),
            pltpu.VMEM((freqs, n_apt, n_rcv * tile, width), jnp.bfloat16),
            pltpu.VMEM((n_apt - 1, freqs, n_rcv * tile, width), jnp.bfloat16),
            dma((3,)),
            dma((freqs,)),
            dma((2, chunks)),
            dma((chunks, n_freq)),
            dma((chunks, n_freq)),
            dma((chunks, n_apt)),
            dma((chunks, n_apt)),
            dma((chunks, 4)),
            dma((chunks, 4)),
            dma((freqs // 2, n_apt - 1, 2)),
            dma((freqs // 2, n_apt - 1, 2)),
        ],
        compiler_params=pltpu.CompilerParams(
            collective_id=0, has_side_effects=True, vmem_limit_bytes=56 * 1024 * 1024
        ),
    )(lists, block_ids, taper_ids, windows(length), green_traces)
    return result.reshape(freqs, n_rcv * shots, parts, width).transpose(1, 0, 2, 3)


def solution(mesh):
    sizes = (mesh.shape["freq"], mesh.shape["apt"], mesh.shape["rcv"])
    return jax.shard_map(
        functools.partial(on_device, sizes),
        mesh=mesh,
        in_specs=(
            P(("apt", "rcv", "freq"), None, None, None, None),
            P(("apt", "rcv"), None),
            P(("apt", "rcv"), None),
            P("freq", None, "apt", "rcv"),
        ),
        out_specs=P("apt", "freq", None, "rcv"),
        check_vma=False,
    )
```

time: 342 us -> 128 us (0.37)
  waiting for transfers between devices: 196 us -> 0 us
  Pallas kernels: 0 us -> 123 us
  blocking collectives: 45.6 us -> 0 us
  matrix products: 43.6 us -> 0 us
  local copies, waits for them, and re-layouts: 26.1 us -> 3.56 us
  between operations: 13.5 us -> 0.02 us
  other arithmetic: 9.68 us -> 0.75 us
  starting transfers between devices: 4.68 us -> 0 us
    pallas_call x0 -> x1, Pallas kernels: none -> 123 us  [on_device(): pl.pallas_call(functools.partial(kernel, sizes), out_shape=jax.ShapeDtype...]
    all_gather x1 -> x0, waiting for transfers between devices: 94.1 us -> none  [on_device(): lax.all_gather(tapered, ('apt', 'rcv'), axis=0, tiled=True)]
    reduce_scatter x1 -> x0, waiting for transfers between devices: 92.2 us -> none  [on_device(): lax.psum_scatter(jnp.stack([real_sum, imag_sum], axis=2).astype(jnp.bfloa...]
    all_gather x1 -> x0, blocking collectives: 45.6 us -> none  [on_device(): lax.all_gather(block_ids, ('apt', 'rcv'), axis=0, tiled=True)]
    dot_general x5 -> x0, matrix products: 43.6 us -> none  [the longest x4 33 us: product(): jnp.einsum('sfk,fkr->sfr', left, right, preferred_element_type=jnp.float32)]
    slice x1 -> x0, local copies, waits for them, and re-layouts: 11.1 us -> none  [on_device(): imag_part = aperture[:, :, 1]]
    all_to_all x1 -> x0, waiting for transfers between devices: 9.32 us -> none  [on_device(): lax.all_to_all(shot_lists, 'freq', split_axis=1, concat_axis=0, tiled=True)]
    reshape x1 -> x2, local copies, waits for them, and re-layouts: 11.7 us -> 3.55 us  [on_device(): result.reshape(freqs, n_rcv * shots, parts, width).transpose(1, 0, 2, 3)]
  transfers between devices with their start and end apart: 3 -> 0, of which waited for: 3 -> 0; matrix products, arithmetic and copies ran while one was open for 0% -> 0% of each run, Pallas kernels for 0% -> 0%
where the time goes in v2:
time: 128 us
  Pallas kernels  123 us (96%)
  local copies, waits for them, and re-layouts  3.56 us (3%)
    pallas_call x1, Pallas kernels, on_device(): pl.pallas_call(functools.partial(kernel, sizes), out_shape=jax.ShapeDtype...  123 us
    reshape x2, local copies, waits for them, and re-layouts, on_device(): result.reshape(freqs, n_rcv * shots, parts, width).transpose(1, 0, 2, 3)  3.55 us

profile of v2, /device:TPU:32, one launch (start us, length us, event | category | flops | bytes accessed | tf_op | source)
XLA Modules:
  0.0 127.8 jit_solution(1163994076795633479)
XLA Ops:
  0.1 0.7 pad_maximum_fusion.shape
  0.8 123.4 %shard_map.46 = bf16[16,64,512]{2,1,0:T(8,128)(2,1)} custom-call(bf16[128,16,128]{2,1,0:T(8,128)(2,1)} %bitcast.5, s32[8,8]{1,0:T(8,128)} %ids.1, s32[8,8]{1,0:T(8,128)} %tapers.1, f32[4,128]{1,0:T(4,128)} %pad_maximum_fusion.shape, bf16[16,2,256,512]{3,2,1,0:T(8,128)(2,1)} %green.1), custom_call_target="tpu_custom_call" | custom-call | tf_op jit(solution)/shard_map/pallas_call | solution.py:319
  124.2 1.5 %reshape.37 = bf16[16,32,2,512]{3,2,1,0:T(2,128)(2,1)S(1)} reshape(bf16[16,64,512]{2,1,0:T(8,128)(2,1)} %shard_map.46) | data formatting | bytes 2097152 | tf_op jit(solution)/shard_map/reshape | solution.py:358
  125.7 2.1 %copy.7 = bf16[16,32,2,512]{3,2,0,1:T(2,128)(2,1)} copy(bf16[16,32,2,512]{3,2,1,0:T(2,128)(2,1)S(1)} %reshape.37) | data formatting | bytes 2097152 | tf_op jit(solution)/shard_map/reshape | solution.py:358
  (3 shorter events, 0.1 us)

commit v3 on v2

--- a/solution.py
+++ b/solution.py
@@ -265,7 +265,8 @@
                 partial[f, goal] = value
                 ring_copy(p, t, way).start()
             else:
-                out[f] = value
+                for k in range(out.shape[1]):
+                    out[f, k] = value[:, k * out.shape[3] : (k + 1) * out.shape[3]]
 
     going = {}
 
@@ -318,7 +319,7 @@
     dma = pltpu.SemaphoreType.DMA
     result = pl.pallas_call(
         functools.partial(kernel, sizes),
-        out_shape=jax.ShapeDtypeStruct((freqs, n_rcv * tile, width), jnp.bfloat16),
+        out_shape=jax.ShapeDtypeStruct((freqs, width // length, n_rcv * tile, length), jnp.bfloat16),
         in_specs=[
             pl.BlockSpec(memory_space=pl.ANY),
             pl.BlockSpec(memory_space=pl.ANY),
@@ -355,7 +356,8 @@
             collective_id=0, has_side_effects=True, vmem_limit_bytes=56 * 1024 * 1024
         ),
     )(lists, block_ids, taper_ids, windows(length), green_traces)
-    return result.reshape(freqs, n_rcv * shots, parts, width).transpose(1, 0, 2, 3)
+    result = result.reshape(freqs, width // length, n_rcv * shots, parts, length)
+    return result.transpose(2, 0, 3, 1, 4).reshape(n_rcv * shots, freqs, parts, width)
 
 
 def solution(mesh):

time: 128 us -> 128 us (level)
    transpose x0 -> x1, local copies, waits for them, and re-layouts: none -> 2.58 us  [on_device(): result.transpose(2, 0, 3, 1, 4).reshape(n_rcv * shots, freqs, parts, width)]
    reshape x2 -> x1, local copies, waits for them, and re-layouts: 3.55 us -> 1.22 us  [on_device(): result.transpose(2, 0, 3, 1, 4).reshape(n_rcv * shots, freqs, parts, width)]
where the time goes in v3:
time: 128 us
  Pallas kernels  123 us (96%)
  local copies, waits for them, and re-layouts  3.8 us (3%)
    pallas_call x1, Pallas kernels, on_device(): pl.pallas_call(functools.partial(kernel, sizes), out_shape=jax.ShapeDtype...  123 us
    transpose x1, local copies, waits for them, and re-layouts, on_device(): result.transpose(2, 0, 3, 1, 4).reshape(n_rcv * shots, freqs, parts, width)  2.58 us

profile of v3, /device:TPU:32, one launch (start us, length us, event | category | flops | bytes accessed | tf_op | source)
XLA Modules:
  0.0 128.0 jit_solution(7209731343185589326)
XLA Ops:
  0.1 0.7 pad_maximum_fusion.shape
  0.8 123.4 %shard_map.46 = bf16[16,4,64,128]{3,2,1,0:T(8,128)(2,1)} custom-call(bf16[128,16,128]{2,1,0:T(8,128)(2,1)} %bitcast.6, s32[8,8]{1,0:T(8,128)} %ids.1, s32[8,8]{1,0:T(8,128)} %tapers.1, f32[4,128]{1,0:T(4,128)} %pad_maximum_fusion.shape, bf16[16,2,256,512]{3,2,1,0:T(8,128)(2,1)} %green.1), custom_call_target="tpu_custom_call" | custom-call | tf_op jit(solution)/shard_map/pallas_call | solution.py:320
  124.2 2.6 %copy.5 = bf16[32,16,2,4,128]{4,3,2,1,0:T(4,128)(2,1)S(1)} copy(bf16[32,16,2,4,128]{4,2,0,3,1:T(2,128)(2,1)} %bitcast.5) | data formatting | bytes 2097152 | tf_op jit(solution)/shard_map/transpose | solution.py:360
  126.8 1.2 reshape.41
  (3 shorter events, 0.1 us)
